TPU v7x, 32 devices: a whole 2x2x4 slice. The times are simulated.
32 devices in a mesh: group: 2 (over x), tm: 4 (over y, core), inline: 4 (over z).
Axes of the slice: x: 2, y: 2, z: 4, core: 2. Of those that a mesh axis runs over, the one named last changes fastest.
Arguments:
- near_trace: float32 [128, 512], P(('group', 'inline'), 'tm'), parts along dimension 0, may hold values from -1.5 to 1.5
- far_trace: float32 [128, 512], P(('group', 'inline'), 'tm'), parts along dimension 0, may hold values from -1.5 to 1.5
- inline_weight: int32 [128, 512], P(('group', 'inline'), 'tm'), parts along dimension 0, may hold values from 0 to 15
- time_weight: int32 [128, 512], P(('group', 'inline'), 'tm'), parts along dimension 0, may hold values from 0 to 15
- lag_low: int32 [128], P(('group', 'inline')), parts along dimension 0, may hold values from 0 to 15
- lag_high: int32 [128], P(('group', 'inline')), parts along dimension 0, may hold values from 48 to 63
- strain: int32 [16], P(('group', 'tm')), parts along dimension 0, may hold values from 1 to 3
Outputs:
- accumulated: float32 [64, 128, 512], P(None, ('group', 'inline'), 'tm'), parts along dimension 1
There are 2 independent parts, one for each index of `group`. A program takes and returns all parts, laid end to end along the dimension named above; each array names one. Nothing has to cross between parts.
All inputs are finite; a program needn't handle non-finite values.
Results may differ from a plain program's by a relative error of at most 0.0003.
Values sent between devices are 32-bit elements; how exact they have to be, the bound alone decides.
A program may use at most 64 MiB of HBM per device.

v0:
```python
import functools

import jax
import jax.numpy as jnp
from jax import lax
from jax.experimental import pallas as pl
from jax.experimental.pallas import tpu as pltpu
from jax.sharding import PartitionSpec as P

L = 64
STRETCH = 64
ITERS = 10

BIG = 1000000000.0
PENALTY = 2.0
FACE_SCALE = 0.016

SUB = 8
LANES = 128


def segments(width, reach, chunk_len):
    cuts = {0, width}
    cuts |= set(range(0, width, STRETCH))
    cuts |= {c * chunk_len - reach for c in range(1, -(-(width + reach) // chunk_len))}
    cuts = sorted(x for x in cuts if 0 <= x <= width)
    return list(zip(cuts[:-1], cuts[1:]))


OFFSETS = [(di, dj) for di in (-1, 0, 1) for dj in (-1, 0, 1) if (di, dj) != (0, 0)]


def slot_of(di, dj):
    return (di + 1) * 3 + dj + 1


def kernel(
    dims,
    far_in,
    near_in,
    inline_in,
    time_in,
    bounds_in,
    strain_ref,
    out_ref,
    trace_ref,
    weight_ref,
    trace_recv,
    weight_recv,
    time_ref,
    far_ref,
    near_ref,
    face_ref,
    m_ref,
    y_ref,
    low_ref,
    send_ref,
    enter_ref,
    local_sems,
    send_sems,
    recv_sems,
    send_sem,
    recv_sem,
):
    rows, width, reach, classes, own, side_pairs, pitch, chunks, chunk_len, count, count_in = dims
    groups = L // SUB
    half = L // 2
    me = lax.axis_index("tm")
    here_in = lax.axis_index("inline")

    def present(di, dj):
        ok = None
        for step, place, total in ((di, here_in, count_in), (dj, me, count)):
            if step:
                inside = (place + step >= 0) & (place + step < total)
                ok = inside if ok is None else ok & inside
        return ok

    def device(di, dj):
        return {
            "inline": lax.clamp(0, here_in + di, count_in - 1),
            "tm": lax.clamp(0, me + dj, count - 1),
        }

    local = [
        pltpu.make_async_copy(source, target, local_sems.at[k])
        for k, (source, target) in enumerate(
            (
                (far_in, trace_ref.at[0]),
                (near_in, trace_ref.at[1]),
                (inline_in, weight_ref.at[0]),
                (time_in, weight_ref.at[1]),
                (bounds_in, weight_ref.at[2]),
            )
        )
    ]
    for copy in local:
        copy.start()

    barrier = pltpu.get_barrier_semaphore()
    for di, dj in OFFSETS:

        @pl.when(present(di, dj))
        def _():
            pl.semaphore_signal(
                barrier, inc=1, device_id=device(di, dj), device_id_type=pl.DeviceIdType.MESH
            )

    beside = [
        1 + (place > 0).astype(jnp.int32) + (place < total - 1).astype(jnp.int32)
        for place, total in ((here_in, count_in), (me, count))
    ]
    pl.semaphore_wait(barrier, beside[0] * beside[1] - 1)

    def halo_copies(di, dj):
        target = slot_of(-di, -dj)
        return [
            pltpu.make_async_remote_copy(
                src_ref=source,
                dst_ref=landing.at[target],
                send_sem=send_sems.at[kind, slot_of(di, dj)],
                recv_sem=recv_sems.at[kind, target],
                device_id=device(di, dj),
                device_id_type=pl.DeviceIdType.MESH,
            )
            for kind, (source, landing) in enumerate(
                ((trace_ref, trace_recv), (weight_ref, weight_recv))
            )
        ]

    for copy in local:
        copy.wait()

    for di, dj in OFFSETS:

        @pl.when(present(di, dj))
        def _():
            for copy in halo_copies(di, dj):
                copy.start()

        @pl.when(jnp.logical_not(present(di, dj)))
        def _():
            trace_recv[slot_of(di, dj)] = jnp.zeros(trace_ref.shape, jnp.float32)
            weight_recv[slot_of(di, dj)] = jnp.zeros(weight_ref.shape, jnp.int32)

    for di, dj in OFFSETS:

        @pl.when(present(di, dj))
        def _():
            for copy in halo_copies(-di, -dj):
                copy.wait_recv()

    stacked = 3 * own

    def block(field, dj, parity):
        parts = []
        for di in (-1, 0, 1):
            pick = pl.ds(parity, own, stride=classes)
            own_ref, landing = (trace_ref, trace_recv) if field < 2 else (weight_ref, weight_recv)
            if di == 0 and dj == 0:
                cells = own_ref[field % 2 if field < 4 else 2, pick, :]
            else:
                cells = landing[slot_of(di, dj), field % 2 if field < 4 else 2, pick, :]
            parts.append(cells.astype(jnp.float32))
        return parts

    for pair in range(2):
        for dj in (-1, 0, 1):
            parts = []
            for field in (2 * pair, 2 * pair + 1):
                for parity in range(classes):
                    parts += block(field, dj, parity)
            tall = jnp.concatenate(parts, axis=0)
            time_ref[pair, (dj + 1) * width : (dj + 2) * width, 0 : tall.shape[0]] = (
                jnp.transpose(tall)
            )

    line = lax.broadcasted_iota(jnp.int32, (1, LANES), 1)
    spot = line % pitch
    live = line < chunks * pitch
    first_time = width - reach

    def pack(pair, start, length, lane_off, step):
        size = -(-length // SUB) * SUB
        result = None
        for c in range(chunks):
            base = start + c * step
            x = time_ref[pair, base : base + size, :]
            x = pltpu.roll(x, (c * pitch - lane_off) % LANES, 1)
            result = x if c == 0 else jnp.where(line >= c * pitch, x, result)
        return jnp.where(live, result, 0.0), size

    skip = own - side_pairs
    span = own + 2 * side_pairs
    inline_rows = []
    for e in range(classes):
        far, size = pack(0, first_time - half, chunk_len + L, e * stacked + skip, chunk_len)
        far_ref[e, 0:size] = far
        near, size = pack(
            0, first_time, chunk_len, (classes + e) * stacked + skip, chunk_len
        )
        near_ref[e, 0:size] = near
        inline_rows.append(pack(1, first_time, chunk_len, e * stacked + skip, chunk_len)[0])
        time_off = (classes + e) * stacked + skip
        time_now = pack(1, first_time, chunk_len, time_off, chunk_len)[0]
        time_next = pack(1, first_time + 1, chunk_len, time_off, chunk_len)[0]
        face_ref[classes + 1 + e, 0:size] = FACE_SCALE * jnp.minimum(time_now, time_next)
    for e in range(classes):
        if e < classes - 1:
            other, inner = inline_rows[e + 1], span
        else:
            other, inner = pltpu.roll(inline_rows[0], LANES - 1, 1), span - 1
        face = jnp.where(spot < inner, FACE_SCALE * jnp.minimum(inline_rows[e], other), 0.0)
        face = jnp.where(live, face, 0.0)
        face_ref[e, 0:size] = face
        if e == classes - 1:
            face_ref[classes, 0:size] = pltpu.roll(face, 1, 1)

    sub = lax.broadcasted_iota(jnp.int32, (SUB, LANES), 0)
    extra = []
    for e in range(classes):
        marks = jnp.transpose(jnp.concatenate(block(4, 0, e) * 2, axis=0))[0:SUB]
        marks = jnp.concatenate(
            [marks, jnp.zeros((SUB, LANES - marks.shape[1]), jnp.float32)], axis=1
        )
        bounds = None
        for c in range(chunks):
            x = pltpu.roll(marks, (c * pitch - skip) % LANES, 1)
            bounds = x if c == 0 else jnp.where(line >= c * pitch, x, bounds)
        lane_low, lane_high = bounds[0:1], bounds[1:2]
        for v in range(groups):
            lag = (sub * groups + v).astype(jnp.float32)
            extra.append(jnp.where((lag < lane_low) | (lag > lane_high), PENALTY, 0.0))

    for e in range(classes):

        def build(j, carry):
            near = near_ref[e, pl.ds(j, 1), :]
            for v in range(groups):
                shifted = far_ref[e, pl.ds(j + v, SUB, stride=groups), :]
                diff = near - shifted
                m_ref[e, j, v] = diff * diff + extra[e * groups + v]
            return carry

        lax.fori_loop(0, chunk_len, build, 0, unroll=5)

    last = chunk_len - 1

    def sweep(k, carry):
        for begin in range(0, groups, 4):
            picks = [(e, v) for e in range(classes) for v in range(begin, begin + 4)]
            first = {p: m_ref[p[0], 0, p[1]] for p in picks}
            flux = {}
            for p in picks:
                e, v = p
                wrapped = pltpu.roll(first[p], LANES - pitch, 1)
                m_ref[e, chunk_len, v] = wrapped
                b_last = face_ref[classes + 1 + e, pl.ds(last, 1), :]
                flux[p] = pltpu.roll(b_last * (wrapped - m_ref[e, last, v]), pitch, 1)

            def cell(j, state):
                here, before = state
                here = dict(zip(picks, here))
                before = dict(zip(picks, before))
                a_rows = [face_ref[e, pl.ds(j, 1), :] for e in range(classes + 1)]
                b_rows = [face_ref[classes + 1 + e, pl.ds(j, 1), :] for e in range(classes)]
                nexts, fluxes = [], []
                links = {}
                for e, v in picks:
                    if e < classes - 1:
                        links[e, v] = a_rows[e] * (here[e + 1, v] - here[e, v])
                    else:
                        up = pltpu.roll(here[0, v], LANES - 1, 1)
                        links[e, v] = a_rows[e] * (up - here[e, v])
                        down = pltpu.roll(here[e, v], 1, 1)
                        links[-1, v] = a_rows[classes] * (here[0, v] - down)
                for p in picks:
                    e, v = p
                    ahead = m_ref[e, j + 1, v]
                    along = b_rows[e] * (ahead - here[p])
                    m_ref[e, j, v] = ((here[p] + links[e, v]) - links[e - 1, v]) + (
                        along - before[p]
                    )
                    nexts.append(ahead)
                    fluxes.append(along)
                return nexts, fluxes

            lax.fori_loop(
                0,
                chunk_len,
                cell,
                ([first[p] for p in picks], [flux[p] for p in picks]),
                unroll=chunk_len,
            )
        return carry

    lax.fori_loop(0, ITERS, sweep, 0)

    owned = (spot >= side_pairs) & (spot < side_pairs + own) & live

    def merge(j, carry):
        for v in range(groups):
            other = pltpu.roll(m_ref[1, j, v], own, 1)
            m_ref[0, j, v] = jnp.where(owned, m_ref[0, j, v], other)
        return carry

    if classes == 2:
        lax.fori_loop(0, chunk_len, merge, 0, unroll=5)

    state_copy = pltpu.make_async_remote_copy(
        src_ref=send_ref,
        dst_ref=enter_ref,
        send_sem=send_sem,
        recv_sem=recv_sem,
        device_id={"tm": lax.min(me + 1, count - 1)},
        device_id_type=pl.DeviceIdType.MESH,
    )

    @pl.when(me == 0)
    def _():
        enter_ref[...] = jnp.zeros(enter_ref.shape, jnp.float32)

    @pl.when(me > 0)
    def _():
        state_copy.wait_recv()

    state = [enter_ref[v] for v in range(groups)]
    lane = lax.broadcasted_iota(jnp.int32, (SUB, LANES), 1)
    at_low = sub == 0
    at_high = sub == SUB - 1
    chunk_now = 0
    for start, stop in segments(width, reach, chunk_len):
        chunk = (start + reach) // chunk_len
        if chunk != chunk_now:
            state = [pltpu.roll(x, pitch, 1) for x in state]
            chunk_now = chunk
        radius = strain_ref[start // STRETCH]
        gate2 = jnp.full((SUB, LANES), jnp.where(radius >= 2, -BIG, BIG), jnp.float32)
        gate3 = jnp.full((SUB, LANES), jnp.where(radius >= 3, -BIG, BIG), jnp.float32)
        mine = lax.rem(lane + (LANES - side_pairs) + LANES - chunk * pitch, LANES) < rows

        def advance(j, x):
            wide = {v: x[v] for v in range(groups)}
            for k in range(1, 4):
                wide[-k] = jnp.where(at_low, BIG, pltpu.roll(x[groups - k], 1, 0))
                wide[groups - 1 + k] = jnp.where(at_high, BIG, pltpu.roll(x[k - 1], SUB - 1, 0))
            pair = {v: jnp.minimum(wide[v], wide[v + 1]) for v in range(-1, groups)}
            new = []
            for v in range(groups):
                near3 = jnp.minimum(pair[v - 1], pair[v])
                two = jnp.maximum(jnp.minimum(wide[v - 2], wide[v + 2]), gate2)
                three = jnp.maximum(jnp.minimum(wide[v - 3], wide[v + 3]), gate3)
                total = m_ref[0, j, v] + jnp.minimum(near3, jnp.minimum(two, three))
                if chunk == 0:
                    y_ref[j, v] = total
                else:
                    y_ref[j, v] = jnp.where(mine, total, y_ref[j, v])
                new.append(total)
            return new

        base = chunk * chunk_len - reach
        state = lax.fori_loop(start - base, stop - base, advance, state, unroll=stop - start)

    @pl.when(me < count - 1)
    def _():
        for v in range(groups):
            send_ref[v] = pltpu.roll(state[v], (LANES - chunk_now * pitch) % LANES, 1)
        state_copy.start()

    def least(j, carry):
        low = y_ref[j, 0]
        for v in range(1, groups):
            low = jnp.minimum(low, y_ref[j, v])
        low = jnp.min(low, axis=0, keepdims=True)
        low_ref[pl.ds(j, 1), :] = low
        return carry

    lax.fori_loop(0, chunk_len, least, 0, unroll=5)

    for lag in range(L):
        sub_index, v = lag // groups, lag % groups
        cells = y_ref[0:chunk_len, v, sub_index, :] - low_ref[0:chunk_len, :]
        flat = jnp.transpose(cells)
        flat = jnp.concatenate([flat, flat[0 : 2 * SUB]], axis=0)
        for e in range(classes):
            parts = []
            for c in range(chunks):
                begin = max(reach - c * chunk_len, 0)
                end = min(width + reach - c * chunk_len, chunk_len)
                if end > begin:
                    at = c * pitch + side_pairs + e * own
                    parts.append(flat[at : at + own, begin:end])
            out_ref[lag, pl.ds(e, own, stride=classes), :] = jnp.concatenate(parts, axis=1)

    @pl.when(me < count - 1)
    def _():
        state_copy.wait_send()

    for di, dj in OFFSETS:

        @pl.when(present(di, dj))
        def _():
            for copy in halo_copies(di, dj):
                copy.wait_send()


def per_device(near_trace, far_trace, inline_weight, time_weight, lag_low, lag_high, strain):
    rows, width = near_trace.shape
    reach = ITERS
    groups = L // SUB
    classes = 2
    own = rows // classes
    side_pairs = -(-reach // classes)
    pitch = -(-(rows + side_pairs) // 1)
    chunks = LANES // pitch
    chunk_len = -(-(width + 2 * reach) // chunks)
    count = lax.axis_size("tm")
    count_in = lax.axis_size("inline")

    mark = lax.broadcasted_iota(jnp.int32, (rows, width), 1)
    bounds = jnp.where(mark == 0, lag_low[:, None], lag_high[:, None])
    vmem = pl.BlockSpec(memory_space=pltpu.VMEM)
    dims = (
        rows,
        width,
        reach,
        classes,
        own,
        side_pairs,
        pitch,
        chunks,
        chunk_len,
        count,
        count_in,
    )
    whole = -(-chunk_len // SUB) * SUB
    deep = -(-(chunk_len + L) // SUB) * SUB
    return pl.pallas_call(
        functools.partial(kernel, dims),
        out_shape=jax.ShapeDtypeStruct((L, rows, width), jnp.float32),
        in_specs=[pl.BlockSpec(memory_space=pl.ANY)] * 5
        + [pl.BlockSpec(memory_space=pltpu.SMEM)],
        out_specs=vmem,
        scratch_shapes=[
            pltpu.VMEM((2, rows, width), jnp.float32),
            pltpu.VMEM((3, rows, width), jnp.int32),
            pltpu.VMEM((9, 2, rows, width), jnp.float32),
            pltpu.VMEM((9, 3, rows, width), jnp.int32),
            pltpu.VMEM((2, 3 * width, LANES), jnp.float32),
            pltpu.VMEM((classes, deep, LANES), jnp.float32),
            pltpu.VMEM((classes, whole, LANES), jnp.float32),
            pltpu.VMEM((2 * classes + 1, whole, LANES), jnp.float32),
            pltpu.VMEM((classes, chunk_len + 1, groups, SUB, LANES), jnp.float32),
            pltpu.VMEM((whole, groups, SUB, LANES), jnp.float32),
            pltpu.VMEM((whole, LANES), jnp.float32),
            pltpu.VMEM((groups, SUB, LANES), jnp.float32),
            pltpu.VMEM((groups, SUB, LANES), jnp.float32),
            pltpu.SemaphoreType.DMA((5,)),
            pltpu.SemaphoreType.DMA((2, 9)),
            pltpu.SemaphoreType.DMA((2, 9)),
            pltpu.SemaphoreType.DMA,
            pltpu.SemaphoreType.DMA,
        ],
        compiler_params=pltpu.CompilerParams(collective_id=0, has_side_effects=True),
    )(far_trace, near_trace, inline_weight, time_weight, bounds, strain)


def solution(mesh):
    return jax.shard_map(
        per_device,
        mesh=mesh,
        in_specs=(
            P(("group", "inline"), "tm"),
            P(("group", "inline"), "tm"),
            P(("group", "inline"), "tm"),
            P(("group", "inline"), "tm"),
            P(("group", "inline")),
            P(("group", "inline")),
            P(("group", "tm")),
        ),
        out_specs=P(None, ("group", "inline"), "tm"),
        check_vma=False,
    )
```

profile of v0, /device:TPU:5, one launch (start us, length us, event | category | flops | bytes accessed | tf_op | source)
XLA Modules:
  0.0 34.4 jit_solution(9471891749458498233)
XLA Ops:
  0.0 0.0 copy-start
  0.0 0.0 copy-start.1
  0.0 0.6 %copy-done = s32[16]{0:T(128)S(1)} copy-done((s32[16]{0:T(128)S(1)}, s32[16]{0:T(128)}, u32[]{:S(2)}) %copy-start) | copy-done | bytes 88
  0.7 0.0 copy-done.1
  0.7 0.7 %broadcast_select_fusion.bounds_in = s32[16,128]{1,0:T(8,128)} fusion(s32[16]{0:T(128)S(1)} %copy-done, s32[16]{0:T(128)S(1)} %copy-done.1, pred[128]{0:T(512)(128)(4,1)S(1)} %iota_compare_fusion), kind=kLoop, calls=%fused_computation | loop fusion | flops 2048 | bytes 8448 | tf_op jit(solution)/shard_map/jit(_where)/select_n | solution.py:421
  1.3 31.1 %shard_map.73 = f32[64,16,128]{2,1,0:T(8,128)} custom-call(f32[16,128]{1,0:T(8,128)} %far_in.1, f32[16,128]{1,0:T(8,128)} %near_in.1, s32[16,128]{1,0:T(8,128)} %inline_in.1, s32[16,128]{1,0:T(8,128)} %time_in.1, s32[16,128]{1,0:T(8,128)} %broadcast_select_fusion.bounds_in, s32[2]{0:T(128)} %strain_ref.1), custom_call_target="tpu_custom_call" | custom-call | tf_op jit(solution)/shard_map/pallas_call | solution.py:438
  32.5 1.9 %copy.9 = f32[64,16,128]{2,1,0:T(8,128)} copy(f32[64,16,128]{2,1,0:T(8,128)} %shard_map.73) | data formatting | bytes 1048576
  (1 shorter events, 0.0 us)
Async XLA Ops:
  0.0 0.7 %copy-start = (s32[16]{0:T(128)S(1)}, s32[16]{0:T(128)}, u32[]{:S(2)}) copy-start(s32[16]{0:T(128)} %param.12) | copy-start | bytes 196
  0.0 0.7 %copy-start.1 = (s32[16]{0:T(128)S(1)}, s32[16]{0:T(128)}, u32[]{:S(2)}) copy-start(s32[16]{0:T(128)} %param.11) | copy-start | bytes 196
where the time goes:
time: 34.6 us; the launch traced here: 34.4 us
  Pallas kernels  31.1 us (90%)
  local copies, waits for them, and re-layouts  2.53 us (7%)
  other arithmetic  0.67 us (2%)
    pallas_call x1, Pallas kernels, per_device(): pl.pallas_call(functools.partial(kernel, dims), out_shape=jax.ShapeDtypeS...  31.1 us
    unnamed x5, local copies, waits for them, and re-layouts  2.53 us

commit v1 on v0

v1 whole, which is shorter than its diff:
```python
import functools

import jax
import jax.numpy as jnp
from jax import lax
from jax.experimental import pallas as pl
from jax.experimental.pallas import tpu as pltpu
from jax.sharding import PartitionSpec as P

L = 64
STRETCH = 64
ITERS = 10

BIG = 1000000000.0
PENALTY = 2.0
FACE_SCALE = 0.016

SUB = 8
LANES = 128
GROUPS = L // SUB
HALF = L // 2
REACH = ITERS
PITCH = LANES // GROUPS
SHIFTS = 3

OFFSETS = [(di, dj) for di in (-1, 0, 1) for dj in (-1, 0, 1) if (di, dj) != (0, 0)]


def slot_of(di, dj):
    return (di + 1) * 3 + dj + 1


def roll(x, shift, axis=1):
    shift %= x.shape[axis]
    return pltpu.roll(x, shift, axis) if shift else x


def kernel(
    dims,
    far_in,
    near_in,
    inline_in,
    time_in,
    low_in,
    high_in,
    strain_in,
    y_ref,
    trace_ref,
    weight_ref,
    trace_recv,
    weight_recv,
    plain_ref,
    field_ref,
    face_ref,
    far_ref,
    bound_ref,
    m_ref,
    packed_ref,
    loose_ref,
    enter_ref,
    low_ref,
    high_ref,
    strain_ref,
    local_sems,
    send_sems,
    recv_sems,
    send_sem,
    recv_sem,
):
    rows, width, count, count_in, tall, high, chunk, deep = dims
    me = lax.axis_index("tm")
    here_in = lax.axis_index("inline")

    def present(di, dj):
        ok = None
        for step, place, total in ((di, here_in, count_in), (dj, me, count)):
            if step:
                inside = (place + step >= 0) & (place + step < total)
                ok = inside if ok is None else ok & inside
        return ok

    def device(di, dj):
        return {
            "inline": lax.clamp(0, here_in + di, count_in - 1),
            "tm": lax.clamp(0, me + dj, count - 1),
        }

    local = [
        pltpu.make_async_copy(source, target, local_sems.at[k])
        for k, (source, target) in enumerate(
            (
                (far_in, trace_ref.at[0]),
                (near_in, trace_ref.at[1]),
                (inline_in, weight_ref.at[0]),
                (time_in, weight_ref.at[1]),
                (low_in, low_ref),
                (high_in, high_ref),
                (strain_in, strain_ref),
            )
        )
    ]
    for copy in local:
        copy.start()

    line = lax.broadcasted_iota(jnp.int32, (1, LANES), 1)
    barrier = pltpu.get_barrier_semaphore()
    for di, dj in OFFSETS:

        @pl.when(present(di, dj))
        def _():
            pl.semaphore_signal(
                barrier, inc=1, device_id=device(di, dj), device_id_type=pl.DeviceIdType.MESH
            )

    beside = [
        1 + (place > 0).astype(jnp.int32) + (place < total - 1).astype(jnp.int32)
        for place, total in ((here_in, count_in), (me, count))
    ]
    for copy in local:
        copy.wait()
    for r in range(rows):
        weight_ref[2, r : r + 1, :] = jnp.where(line < LANES // 2, low_ref[r], -high_ref[r])

    pl.semaphore_wait(barrier, beside[0] * beside[1] - 1)

    def part(di):
        return {-1: slice(0, REACH), 0: slice(0, rows), 1: slice(rows - REACH, rows)}[di]

    def halo_copies(di, dj):
        target = slot_of(-di, -dj)
        cut = part(di)
        planes = 3 if dj == 0 else 2
        return [
            pltpu.make_async_remote_copy(
                src_ref=source.at[0:depth, cut, :],
                dst_ref=landing.at[target, 0:depth, cut, :],
                send_sem=send_sems.at[kind, slot_of(di, dj)],
                recv_sem=recv_sems.at[kind, target],
                device_id=device(di, dj),
                device_id_type=pl.DeviceIdType.MESH,
            )
            for kind, (source, landing, depth) in enumerate(
                ((trace_ref, trace_recv, 2), (weight_ref, weight_recv, planes))
            )
        ]

    for di, dj in OFFSETS:

        @pl.when(present(di, dj))
        def _():
            for copy in halo_copies(di, dj):
                copy.start()

        @pl.when(jnp.logical_not(present(di, dj)))
        def _():
            trace_recv[slot_of(di, dj)] = jnp.zeros(trace_ref.shape, jnp.float32)
            weight_recv[slot_of(di, dj)] = jnp.zeros(weight_ref.shape, jnp.int32)

    for di, dj in OFFSETS:

        @pl.when(present(di, dj))
        def _():
            for copy in halo_copies(-di, -dj):
                copy.wait_recv()

    def cells(field, di, dj):
        cut = part(-di)
        own_ref, landing = (trace_ref, trace_recv) if field < 2 else (weight_ref, weight_recv)
        plane = field % 2 if field < 4 else 2
        if di == 0 and dj == 0:
            x = own_ref[plane, cut, :]
        else:
            x = landing[slot_of(di, dj), plane, cut, :]
        return x.astype(jnp.float32)

    def windows(field, di, before):
        left, own, right = (cells(field, di, dj) for dj in (-1, 0, 1))
        first = roll(jnp.where(line >= width - before, left, own), before)
        second = roll(jnp.where(line >= width - before, own, right), before)
        return first, second

    def ahead_by(first, second, k):
        if k == 0:
            return first, second
        return roll(jnp.where(line < k, second, first), -k), roll(second, -k)

    tops = {-1: 0, 0: REACH, 1: REACH + rows}
    for di in (-1, 0, 1):
        top = tops[di]
        size = REACH if di else rows
        pair = windows(0, di, REACH + HALF)
        for k in range(SHIFTS):
            for tile, x in enumerate(ahead_by(*pair, k)):
                plain_ref[1, tile, k * high + top : k * high + top + size, :] = x
        for tile, x in enumerate(windows(1, di, REACH)):
            plain_ref[0, tile, top : top + size, :] = x
        for tile, x in enumerate(windows(2, di, REACH)):
            plain_ref[2, tile, top : top + size, :] = x
        pair = windows(3, di, REACH)
        for tile, (x, y) in enumerate(zip(pair, ahead_by(*pair, 1))):
            plain_ref[0, tile, 2 * high + top : 2 * high + top + size, :] = (
                FACE_SCALE * jnp.minimum(x, y)
            )
        bound_ref[top : top + size, :] = cells(4, di, 0)
    for tile in range(2):
        plain_ref[0, tile, high : high + tall - 1, :] = FACE_SCALE * jnp.minimum(
            plain_ref[2, tile, 0 : tall - 1, :], plain_ref[2, tile, 1:tall, :]
        )
    for kind in range(2):
        for tile in range(2):
            field_ref[kind, tile * LANES : (tile + 1) * LANES, :] = jnp.transpose(
                plain_ref[kind, tile]
            )
    for c in range(chunk):
        part_c = field_ref[0, pl.ds(c, PITCH, stride=chunk), :]
        face_ref[c] = jnp.transpose(jnp.concatenate([part_c] * GROUPS, axis=0))
    for y in range(0, chunk + SUB - 1, SHIFTS):
        parts = [
            field_ref[1, pl.ds(y + g * SUB, PITCH, stride=chunk), :] for g in range(GROUPS)
        ]
        block = jnp.transpose(jnp.concatenate(parts, axis=0))
        for k in range(SHIFTS):
            if y + k < deep:
                far_ref[pl.ds(y + k, tall, stride=deep), :] = block[
                    k * high : k * high + tall
                ]

    sub = lax.broadcasted_iota(jnp.int32, (SUB, LANES), 0)
    lane = lax.broadcasted_iota(jnp.int32, (SUB, LANES), 1)
    lag = ((lane // PITCH) * SUB + sub).astype(jnp.float32)
    key = jnp.where(lane < LANES // 2, lag, -lag)

    def build(t, carry):
        penalty = jnp.where(key < bound_ref[pl.ds(t, 1), :], PENALTY, 0.0)
        for c in range(chunk):
            near = face_ref[c, pl.ds(t, 1), :]
            diff = near - far_ref[pl.ds(t * deep + c, SUB), :]
            m_ref[t, c] = diff * diff + penalty
        return carry

    lax.fori_loop(0, tall, build, 0, unroll=4)

    for step in range(1, ITERS + 1):
        start, stop = step, tall - step

        def relax(t, state):
            here, before = state
            along = []
            for c in range(chunk):
                after = here[c + 1] if c < chunk - 1 else pltpu.roll(here[0], LANES - 1, 1)
                along.append(face_ref[c, pl.ds(2 * high + t, 1), :] * (after - here[c]))
            back = [pltpu.roll(along[-1], 1, 1)] + along[:-1]
            nexts, fluxes = [], []
            for c in range(chunk):
                ahead = m_ref[t + 1, c]
                across = face_ref[c, pl.ds(high + t, 1), :] * (ahead - here[c])
                m_ref[t, c] = (here[c] + (across - before[c])) + (along[c] - back[c])
                nexts.append(ahead)
                fluxes.append(across)
            return nexts, fluxes

        here = [m_ref[start, c] for c in range(chunk)]
        before = [
            face_ref[c, high + start - 1 : high + start, :] * (here[c] - m_ref[start - 1, c])
            for c in range(chunk)
        ]
        lax.fori_loop(start, stop, relax, (here, before), unroll=stop - start)

    for c in range(chunk):
        block = m_ref[REACH : REACH + rows, c].reshape(LANES, LANES)
        packed_ref[c * LANES : (c + 1) * LANES, :] = jnp.transpose(block)

    def unpack(x):
        return [roll(x, -v) for v in range(GROUPS)]

    spots = [lane % GROUPS == v for v in range(GROUPS)]

    def pack(xs):
        result = xs[0]
        for v in range(1, GROUPS):
            result = jnp.where(spots[v], roll(xs[v], v), result)
        return result

    def loose(index):
        return pl.ds(pl.multiple_of(index * SUB, SUB), SUB)

    @pl.when(me > 0)
    def _():
        def loosen(i, carry):
            for c in range(chunk):
                x = packed_ref[pl.ds(c * LANES + i, SUB, stride=PITCH), :]
                for v, y in enumerate(unpack(x)):
                    loose_ref[loose((i * chunk + c) * GROUPS + v), :] = y
            return carry

        lax.fori_loop(REACH // chunk, (width + REACH - 1) // chunk + 1, loosen, 0)

    last = width - 1
    state_copy = pltpu.make_async_remote_copy(
        src_ref=y_ref.at[last * SUB : (last + 1) * SUB, :],
        dst_ref=enter_ref,
        send_sem=send_sem,
        recv_sem=recv_sem,
        device_id={"tm": lax.min(me + 1, count - 1)},
        device_id_type=pl.DeviceIdType.MESH,
    )

    at_low = sub == 0
    at_high = sub == SUB - 1
    top = GROUPS - 1
    wide3 = [strain_ref[k] >= 3 for k in range(width // STRETCH)]
    wide2 = [strain_ref[k] >= 2 for k in range(width // STRETCH)]

    def advance(x, cost, k):
        wide = {v: x[v] for v in range(GROUPS)}
        for d in range(1, 4):
            wide[-d] = jnp.where(at_low, BIG, pltpu.roll(x[GROUPS - d], 1, 0))
            wide[top + d] = jnp.where(at_high, BIG, pltpu.roll(x[d - 1], SUB - 1, 0))
        pair = {v: jnp.minimum(wide[v], wide[v + 1]) for v in range(-1, GROUPS)}
        gate2 = jnp.full((SUB, LANES), jnp.where(wide2[k], -BIG, BIG), jnp.float32)
        gate3 = jnp.full((SUB, LANES), jnp.where(wide3[k], -BIG, BIG), jnp.float32)
        result = []
        for v in range(GROUPS):
            near3 = jnp.minimum(pair[v - 1], pair[v])
            two = jnp.maximum(jnp.minimum(wide[v - 2], wide[v + 2]), gate2)
            three = jnp.maximum(jnp.minimum(wide[v - 3], wide[v + 3]), gate3)
            result.append(cost[v] + jnp.minimum(near3, jnp.minimum(two, three)))
        return result

    @pl.when(me == 0)
    def _():
        state = [jnp.zeros((SUB, LANES), jnp.float32)] * GROUPS
        for s in range(width):
            x = s + REACH
            cost = unpack(packed_ref[pl.ds((x % chunk) * LANES + x // chunk, SUB, stride=PITCH), :])
            state = advance(state, cost, s // STRETCH)
            if s < last:
                for v in range(GROUPS):
                    loose_ref[loose(s * GROUPS + v), :] = state[v]
        y_ref[last * SUB : (last + 1) * SUB, :] = pack(state)

    @pl.when(me > 0)
    def _():
        state_copy.wait_recv()
        state = unpack(enter_ref[...])
        for s in range(width):
            cost = [loose_ref[loose((s + REACH) * GROUPS + v), :] for v in range(GROUPS)]
            state = advance(state, cost, s // STRETCH)
            y_ref[s * SUB : (s + 1) * SUB, :] = pack(state)

    @pl.when(me < count - 1)
    def _():
        state_copy.start()

    @pl.when(me == 0)
    def _():
        def tighten(s, carry):
            x = [loose_ref[loose(s * GROUPS + v), :] for v in range(GROUPS)]
            y_ref[pl.ds(pl.multiple_of(s * SUB, SUB), SUB), :] = pack(x)
            return carry

        lax.fori_loop(0, last, tighten, 0, unroll=4)

    @pl.when(me < count - 1)
    def _():
        state_copy.wait_send()

    for di, dj in OFFSETS:

        @pl.when(present(di, dj))
        def _():
            for copy in halo_copies(di, dj):
                copy.wait_send()


def spread(dims, y_ref, out_ref, turned_ref):
    rows, width = dims
    least = [None] * rows
    for g in range(SUB):
        block = jnp.transpose(y_ref[pl.ds(g, width, stride=SUB), :])
        turned_ref[g] = block
        for r in range(rows):
            tile = block[r * SUB : (r + 1) * SUB]
            least[r] = tile if g == 0 else jnp.minimum(least[r], tile)
    for r in range(rows):
        low = jnp.min(least[r], axis=0, keepdims=True)
        for g in range(SUB):
            tile = turned_ref[g, r * SUB : (r + 1) * SUB, :] - low
            out_ref[pl.ds(g * SUB * rows + r, SUB, stride=rows), :] = tile


def per_device(near_trace, far_trace, inline_weight, time_weight, lag_low, lag_high, strain):
    rows, width = near_trace.shape
    count = lax.axis_size("tm")
    count_in = lax.axis_size("inline")
    tall = rows + 2 * REACH
    high = -(-tall // SUB) * SUB
    chunk = -(-(width + 2 * REACH) // PITCH)
    deep = -(-(chunk + SUB - 1) // SUB) * SUB
    assert width == LANES and rows * SUB == LANES and SHIFTS * high <= LANES
    assert chunk * PITCH + L <= 2 * LANES and REACH + HALF <= width
    vmem = pl.BlockSpec(memory_space=pltpu.VMEM)
    packed = pl.pallas_call(
        functools.partial(kernel, (rows, width, count, count_in, tall, high, chunk, deep)),
        out_shape=jax.ShapeDtypeStruct((width * SUB, LANES), jnp.float32),
        in_specs=[pl.BlockSpec(memory_space=pltpu.HBM)] * 7,
        out_specs=vmem,
        scratch_shapes=[
            pltpu.VMEM((2, rows, width), jnp.float32),
            pltpu.VMEM((3, rows, width), jnp.int32),
            pltpu.VMEM((9, 2, rows, width), jnp.float32),
            pltpu.VMEM((9, 3, rows, width), jnp.int32),
            pltpu.VMEM((3, 2, LANES, LANES), jnp.float32),
            pltpu.VMEM((2, 2 * LANES, LANES), jnp.float32),
            pltpu.VMEM((chunk, LANES, LANES), jnp.float32),
            pltpu.VMEM((tall * deep, LANES), jnp.float32),
            pltpu.VMEM((high, LANES), jnp.float32),
            pltpu.VMEM((tall, chunk, SUB, LANES), jnp.float32),
            pltpu.VMEM((chunk * LANES, LANES), jnp.float32),
            pltpu.VMEM((chunk * PITCH * GROUPS * SUB, LANES), jnp.float32),
            pltpu.VMEM((SUB, LANES), jnp.float32),
            pltpu.SMEM(lag_low.shape, jnp.int32),
            pltpu.SMEM(lag_high.shape, jnp.int32),
            pltpu.SMEM(strain.shape, jnp.int32),
            pltpu.SemaphoreType.DMA((7,)),
            pltpu.SemaphoreType.DMA((2, 9)),
            pltpu.SemaphoreType.DMA((2, 9)),
            pltpu.SemaphoreType.DMA,
            pltpu.SemaphoreType.DMA,
        ],
        compiler_params=pltpu.CompilerParams(
            collective_id=0, has_side_effects=True, vmem_limit_bytes=24 << 20
        ),
    )(
        *[
            pltpu.with_memory_space_constraint(x, pltpu.HBM)
            for x in (far_trace, near_trace, inline_weight, time_weight, lag_low, lag_high, strain)
        ]
    )
    out = pl.pallas_call(
        functools.partial(spread, (rows, width)),
        out_shape=jax.ShapeDtypeStruct((L * rows, width), jnp.float32),
        in_specs=[vmem],
        out_specs=vmem,
        scratch_shapes=[pltpu.VMEM((SUB, LANES, width), jnp.float32)],
        compiler_params=pltpu.CompilerParams(vmem_limit_bytes=24 << 20),
    )(packed)
    return out.reshape(L, rows, width)


def solution(mesh):
    return jax.shard_map(
        per_device,
        mesh=mesh,
        in_specs=(
            P(("group", "inline"), "tm"),
            P(("group", "inline"), "tm"),
            P(("group", "inline"), "tm"),
            P(("group", "inline"), "tm"),
            P(("group", "inline")),
            P(("group", "inline")),
            P(("group", "tm")),
        ),
        out_specs=P(None, ("group", "inline"), "tm"),
        check_vma=False,
    )
```

time: 34.6 us -> 21.9 us (0.63)
  Pallas kernels: 31.1 us -> 21.7 us
  local copies, waits for them, and re-layouts: 2.53 us -> 0 us
  other arithmetic: 0.67 us -> 0 us
    pallas_call x1 -> x2, Pallas kernels: 31.1 us -> 21.7 us  [the longest x1 20.5 us: per_device(): pl.pallas_call(functools.partial(kernel, (rows, width, count, count_in, t...]
    unnamed x5 -> x0, local copies, waits for them, and re-layouts: 2.53 us -> none
    select_n x1 -> x0, other arithmetic: 0.67 us -> none  [per_device(): bounds = jnp.where(mark == 0, lag_low[:, None], lag_high[:, None])]
where the time goes in v1:
time: 21.9 us; the launch traced here: 21.7 us
  Pallas kernels  21.7 us (99%)
    pallas_call x1, Pallas kernels, per_device(): pl.pallas_call(functools.partial(kernel, (rows, width, count, count_in, t...  20.5 us
    pallas_call x1, Pallas kernels, per_device(): pl.pallas_call(functools.partial(spread, (rows, width)), out_shape=jax.Sh...  1.23 us

profile of v1, /device:TPU:5, one launch (start us, length us, event | category | flops | bytes accessed | tf_op | source)
XLA Modules:
  0.0 21.7 jit_solution(12809711544747590565)
XLA Ops:
  0.0 20.5 %shard_map.73.y_ref = f32[1024,128]{1,0:T(8,128)S(1)} custom-call(f32[16,128]{1,0:T(8,128)} %far_in.1, f32[16,128]{1,0:T(8,128)} %near_in.1, s32[16,128]{1,0:T(8,128)} %inline_in.1, s32[16,128]{1,0:T(8,128)} %time_in.1, s32[16]{0:T(128)} %low_in.1, s32[16]{0:T(128)} %high_in.1, s32[2]{0:T(128)} %strain_in.1), custom_call_target="tpu_custom_call" | custom-call | tf_op jit(solution)/shard_map/pallas_call | solution.py:403
  20.5 1.2 %shard_map.74 = f32[1024,128]{1,0:T(8,128)} custom-call(f32[1024,128]{1,0:T(8,128)S(1)} %shard_map.73.y_ref), custom_call_target="tpu_custom_call" | custom-call | tf_op jit(solution)/shard_map/pallas_call | solution.py:440

commit v2 on v1

--- a/solution.py
+++ b/solution.py
@@ -47,9 +47,12 @@
     y_ref,
     trace_ref,
     weight_ref,
+    pack_ref,
     trace_recv,
     weight_recv,
+    pack_recv,
     plain_ref,
+    inline_ref,
     field_ref,
     face_ref,
     far_ref,
@@ -68,6 +71,8 @@
     recv_sem,
 ):
     rows, width, count, count_in, tall, high, chunk, deep = dims
+    edge = REACH + HALF
+    filled = edge + 3 * REACH
     me = lax.axis_index("tm")
     here_in = lax.axis_index("inline")
 
@@ -119,7 +124,27 @@
     for copy in local:
         copy.wait()
     for r in range(rows):
-        weight_ref[2, r : r + 1, :] = jnp.where(line < LANES // 2, low_ref[r], -high_ref[r])
+        bound_ref[REACH + r : REACH + r + 1, :] = jnp.where(
+            line < LANES // 2, low_ref[r], -high_ref[r]
+        ).astype(jnp.float32)
+
+    def own(field):
+        ref = trace_ref if field < 2 else weight_ref
+        return ref[field % 2].astype(jnp.float32)
+
+    widths = (edge, REACH, REACH, REACH)
+    starts = (0, edge, edge + REACH, edge + 2 * REACH)
+    marks = roll(bound_ref[REACH : REACH + rows, :], (filled + LANES) // 2 - LANES // 2)
+    for side in range(2):
+        result = marks
+        for field in reversed(range(4)):
+            first = 0 if side else width - widths[field]
+            result = jnp.where(
+                line < starts[field] + widths[field],
+                roll(own(field), starts[field] - first),
+                result,
+            )
+        pack_ref[side] = result
 
     pl.semaphore_wait(barrier, beside[0] * beside[1] - 1)
 
@@ -129,55 +154,65 @@
     def halo_copies(di, dj):
         target = slot_of(-di, -dj)
         cut = part(di)
-        planes = 3 if dj == 0 else 2
+        if dj:
+            pairs = ((pack_ref.at[(1 - dj) // 2], pack_recv.at[target]),)
+        else:
+            spot = (1 - di) // 2
+            pairs = (
+                (trace_ref.at[:, cut, :], trace_recv.at[spot, :, cut, :]),
+                (weight_ref.at[:, cut, :], weight_recv.at[spot, :, cut, :]),
+            )
+        if dj and di:
+            pairs = ((pack_ref.at[(1 - dj) // 2, cut, :], pack_recv.at[target, cut, :]),)
         return [
             pltpu.make_async_remote_copy(
-                src_ref=source.at[0:depth, cut, :],
-                dst_ref=landing.at[target, 0:depth, cut, :],
+                src_ref=source,
+                dst_ref=landing,
                 send_sem=send_sems.at[kind, slot_of(di, dj)],
                 recv_sem=recv_sems.at[kind, target],
                 device_id=device(di, dj),
                 device_id_type=pl.DeviceIdType.MESH,
             )
-            for kind, (source, landing, depth) in enumerate(
-                ((trace_ref, trace_recv, 2), (weight_ref, weight_recv, planes))
-            )
+            for kind, (source, landing) in enumerate(pairs)
         ]
 
-    for di, dj in OFFSETS:
+    order = sorted(OFFSETS, key=lambda o: (o[0] == 0, o[1] == 0))
+    for di, dj in order:
 
         @pl.when(present(di, dj))
         def _():
             for copy in halo_copies(di, dj):
                 copy.start()
 
+    for di, dj in OFFSETS:
+
         @pl.when(jnp.logical_not(present(di, dj)))
         def _():
-            trace_recv[slot_of(di, dj)] = jnp.zeros(trace_ref.shape, jnp.float32)
-            weight_recv[slot_of(di, dj)] = jnp.zeros(weight_ref.shape, jnp.int32)
-
-    for di, dj in OFFSETS:
-
+            if dj:
+                pack_recv[slot_of(di, dj)] = jnp.zeros((rows, width), jnp.float32)
+            else:
+                trace_recv[(1 + di) // 2] = jnp.zeros(trace_ref.shape, jnp.float32)
+                weight_recv[(1 + di) // 2] = jnp.zeros(weight_ref.shape, jnp.int32)
+
+    def arrive(di, dj):
         @pl.when(present(di, dj))
         def _():
             for copy in halo_copies(-di, -dj):
                 copy.wait_recv()
 
-    def cells(field, di, dj):
+    def windows(field, di):
         cut = part(-di)
-        own_ref, landing = (trace_ref, trace_recv) if field < 2 else (weight_ref, weight_recv)
-        plane = field % 2 if field < 4 else 2
-        if di == 0 and dj == 0:
-            x = own_ref[plane, cut, :]
+        if di == 0:
+            middle = own(field)
         else:
-            x = landing[slot_of(di, dj), plane, cut, :]
-        return x.astype(jnp.float32)
-
-    def windows(field, di, before):
-        left, own, right = (cells(field, di, dj) for dj in (-1, 0, 1))
-        first = roll(jnp.where(line >= width - before, left, own), before)
-        second = roll(jnp.where(line >= width - before, own, right), before)
-        return first, second
+            landing = trace_recv if field < 2 else weight_recv
+            middle = landing[(1 + di) // 2, field % 2, cut, :].astype(jnp.float32)
+        left, right = (pack_recv[slot_of(di, dj), cut, :] for dj in (-1, 1))
+        n = widths[field]
+        turned = roll(middle, n)
+        first = jnp.where(line < n, roll(left, -starts[field]), turned)
+        rest = jnp.where(line < 2 * n, roll(right, n - starts[field]), 0.0)
+        return first, jnp.where(line < n, turned, rest)
 
     def ahead_by(first, second, k):
         if k == 0:
@@ -185,45 +220,81 @@
         return roll(jnp.where(line < k, second, first), -k), roll(second, -k)
 
     tops = {-1: 0, 0: REACH, 1: REACH + rows}
-    for di in (-1, 0, 1):
-        top = tops[di]
-        size = REACH if di else rows
-        pair = windows(0, di, REACH + HALF)
-        for k in range(SHIFTS):
-            for tile, x in enumerate(ahead_by(*pair, k)):
-                plain_ref[1, tile, k * high + top : k * high + top + size, :] = x
-        for tile, x in enumerate(windows(1, di, REACH)):
-            plain_ref[0, tile, top : top + size, :] = x
-        for tile, x in enumerate(windows(2, di, REACH)):
-            plain_ref[2, tile, top : top + size, :] = x
-        pair = windows(3, di, REACH)
-        for tile, (x, y) in enumerate(zip(pair, ahead_by(*pair, 1))):
-            plain_ref[0, tile, 2 * high + top : 2 * high + top + size, :] = (
-                FACE_SCALE * jnp.minimum(x, y)
-            )
-        bound_ref[top : top + size, :] = cells(4, di, 0)
-    for tile in range(2):
-        plain_ref[0, tile, high : high + tall - 1, :] = FACE_SCALE * jnp.minimum(
-            plain_ref[2, tile, 0 : tall - 1, :], plain_ref[2, tile, 1:tall, :]
-        )
-    for kind in range(2):
-        for tile in range(2):
-            field_ref[kind, tile * LANES : (tile + 1) * LANES, :] = jnp.transpose(
-                plain_ref[kind, tile]
-            )
-    for c in range(chunk):
-        part_c = field_ref[0, pl.ds(c, PITCH, stride=chunk), :]
-        face_ref[c] = jnp.transpose(jnp.concatenate([part_c] * GROUPS, axis=0))
-    for y in range(0, chunk + SUB - 1, SHIFTS):
-        parts = [
-            field_ref[1, pl.ds(y + g * SUB, PITCH, stride=chunk), :] for g in range(GROUPS)
-        ]
-        block = jnp.transpose(jnp.concatenate(parts, axis=0))
-        for k in range(SHIFTS):
-            if y + k < deep:
-                far_ref[pl.ds(y + k, tall, stride=deep), :] = block[
-                    k * high : k * high + tall
-                ]
+    sizes = {-1: REACH, 0: rows, 1: REACH}
+
+    def prepare(bank, parts, links):
+        gap = LANES // SHIFTS // SUB * SUB
+        far_at = dict(zip(parts, (0, -(-REACH // SUB) * SUB)))
+
+        def place(ranges):
+            spots, at = [], 0
+            for start, stop in ranges:
+                at += (start - at) % SUB
+                spots.append((start, stop, at))
+                at += stop - start
+            assert at <= gap
+            return spots
+
+        cell_spots = place([(tops[di], tops[di] + sizes[di]) for di in parts])
+        link_spots = place(links)
+        for di, (_, _, at) in zip(parts, cell_spots):
+            top, size = tops[di], sizes[di]
+            pair = windows(0, di)
+            for k in range(SHIFTS):
+                for tile, x in enumerate(ahead_by(*pair, k)):
+                    begin = k * gap + far_at[di]
+                    plain_ref[bank, 1, tile, begin : begin + size, :] = x
+            for tile, x in enumerate(windows(1, di)):
+                plain_ref[bank, 0, tile, at : at + size, :] = x
+            for tile, x in enumerate(windows(2, di)):
+                inline_ref[tile, top : top + size, :] = x
+            pair = windows(3, di)
+            for tile, (x, y) in enumerate(zip(pair, ahead_by(*pair, 1))):
+                plain_ref[bank, 0, tile, 2 * gap + at : 2 * gap + at + size, :] = (
+                    FACE_SCALE * jnp.minimum(x, y)
+                )
+            if di:
+                low = high_ = None
+                for dj in (-1, 1):
+                    marks = pack_recv[slot_of(di, dj), part(-di), :]
+                    x, y = marks[:, filled : filled + 1], marks[:, LANES - 1 : LANES]
+                    low = x if low is None else jnp.maximum(low, x)
+                    high_ = y if high_ is None else jnp.minimum(high_, y)
+                bound_ref[top : top + size, :] = jnp.where(line < LANES // 2, low, high_)
+        for start, stop, at in link_spots:
+            for tile in range(2):
+                plain_ref[bank, 0, tile, gap + at : gap + at + stop - start, :] = (
+                    FACE_SCALE
+                    * jnp.minimum(
+                        inline_ref[tile, start:stop, :], inline_ref[tile, start + 1 : stop + 1, :]
+                    )
+                )
+        for kind in range(2):
+            for tile in range(2):
+                field_ref[bank, kind, tile * LANES : (tile + 1) * LANES, :] = jnp.transpose(
+                    plain_ref[bank, kind, tile]
+                )
+        for c in range(chunk):
+            piece = field_ref[bank, 0, pl.ds(c, PITCH, stride=chunk), :]
+            block = jnp.transpose(jnp.concatenate([piece] * GROUPS, axis=0))
+            for kind, spots in enumerate((cell_spots, link_spots, cell_spots)):
+                for start, stop, at in spots:
+                    face_ref[c, kind * high + start : kind * high + stop, :] = block[
+                        kind * gap + at : kind * gap + at + stop - start
+                    ]
+        for y in range(0, chunk + SUB - 1, SHIFTS):
+            pieces = [
+                field_ref[bank, 1, pl.ds(y + g * SUB, PITCH, stride=chunk), :]
+                for g in range(GROUPS)
+            ]
+            block = jnp.transpose(jnp.concatenate(pieces, axis=0))
+            for k in range(SHIFTS):
+                if y + k < deep:
+                    for di in parts:
+                        begin = k * gap + far_at[di]
+                        far_ref[pl.ds(tops[di] * deep + y + k, sizes[di], stride=deep), :] = (
+                            block[begin : begin + sizes[di]]
+                        )
 
     sub = lax.broadcasted_iota(jnp.int32, (SUB, LANES), 0)
     lane = lax.broadcasted_iota(jnp.int32, (SUB, LANES), 1)
@@ -238,7 +309,17 @@
             m_ref[t, c] = diff * diff + penalty
         return carry
 
-    lax.fori_loop(0, tall, build, 0, unroll=4)
+    for dj in (-1, 1):
+        arrive(0, dj)
+    prepare(0, (0,), [(REACH, REACH + rows - 1)])
+    lax.fori_loop(REACH, REACH + rows, build, 0, unroll=4)
+
+    for di, dj in OFFSETS:
+        if di:
+            arrive(di, dj)
+    prepare(1, (-1, 1), [(0, REACH), (REACH + rows - 1, tall - 1)])
+    lax.fori_loop(0, REACH, build, 0, unroll=5)
+    lax.fori_loop(REACH + rows, tall, build, 0, unroll=5)
 
     for step in range(1, ITERS + 1):
         start, stop = step, tall - step
@@ -308,23 +389,26 @@
     at_low = sub == 0
     at_high = sub == SUB - 1
     top = GROUPS - 1
-    wide3 = [strain_ref[k] >= 3 for k in range(width // STRETCH)]
-    wide2 = [strain_ref[k] >= 2 for k in range(width // STRETCH)]
+    wide3 = [jnp.full((SUB, LANES), strain_ref[k]) >= 3 for k in range(width // STRETCH)]
+    wide2 = [jnp.full((SUB, LANES), strain_ref[k]) >= 2 for k in range(width // STRETCH)]
+
+    def below(x):
+        return jnp.where(at_low, BIG, pltpu.roll(x, 1, 0))
+
+    def above(x):
+        return jnp.where(at_high, BIG, pltpu.roll(x, SUB - 1, 0))
 
     def advance(x, cost, k):
-        wide = {v: x[v] for v in range(GROUPS)}
-        for d in range(1, 4):
-            wide[-d] = jnp.where(at_low, BIG, pltpu.roll(x[GROUPS - d], 1, 0))
-            wide[top + d] = jnp.where(at_high, BIG, pltpu.roll(x[d - 1], SUB - 1, 0))
-        pair = {v: jnp.minimum(wide[v], wide[v + 1]) for v in range(-1, GROUPS)}
-        gate2 = jnp.full((SUB, LANES), jnp.where(wide2[k], -BIG, BIG), jnp.float32)
-        gate3 = jnp.full((SUB, LANES), jnp.where(wide3[k], -BIG, BIG), jnp.float32)
+        x = [below(x[top])] + x + [above(x[0])]
+        pair = [jnp.minimum(x[v], x[v + 1]) for v in range(GROUPS + 1)]
+        one = [jnp.minimum(pair[v], pair[v + 1]) for v in range(GROUPS)]
+        wide = [below(one[top - 1]), below(one[top])] + one + [above(one[0]), above(one[1])]
+        two = [jnp.minimum(wide[v], wide[v + 2]) for v in range(GROUPS + 2)]
+        three = [jnp.minimum(two[v], two[v + 2]) for v in range(GROUPS)]
         result = []
         for v in range(GROUPS):
-            near3 = jnp.minimum(pair[v - 1], pair[v])
-            two = jnp.maximum(jnp.minimum(wide[v - 2], wide[v + 2]), gate2)
-            three = jnp.maximum(jnp.minimum(wide[v - 3], wide[v + 3]), gate3)
-            result.append(cost[v] + jnp.minimum(near3, jnp.minimum(two, three)))
+            near = jnp.where(wide2[k], two[v + 1], one[v])
+            result.append(cost[v] + jnp.where(wide3[k], three[v], near))
         return result
 
     @pl.when(me == 0)
@@ -398,6 +482,7 @@
     chunk = -(-(width + 2 * REACH) // PITCH)
     deep = -(-(chunk + SUB - 1) // SUB) * SUB
     assert width == LANES and rows * SUB == LANES and SHIFTS * high <= LANES
+    assert REACH + HALF + 3 * REACH < LANES - SUB and REACH <= rows
     assert chunk * PITCH + L <= 2 * LANES and REACH + HALF <= width
     vmem = pl.BlockSpec(memory_space=pltpu.VMEM)
     packed = pl.pallas_call(
@@ -407,11 +492,14 @@
         out_specs=vmem,
         scratch_shapes=[
             pltpu.VMEM((2, rows, width), jnp.float32),
-            pltpu.VMEM((3, rows, width), jnp.int32),
-            pltpu.VMEM((9, 2, rows, width), jnp.float32),
-            pltpu.VMEM((9, 3, rows, width), jnp.int32),
-            pltpu.VMEM((3, 2, LANES, LANES), jnp.float32),
-            pltpu.VMEM((2, 2 * LANES, LANES), jnp.float32),
+            pltpu.VMEM((2, rows, width), jnp.int32),
+            pltpu.VMEM((2, rows, width), jnp.float32),
+            pltpu.VMEM((2, 2, rows, width), jnp.float32),
+            pltpu.VMEM((2, 2, rows, width), jnp.int32),
+            pltpu.VMEM((9, rows, width), jnp.float32),
+            pltpu.VMEM((2, 2, 2, LANES, LANES), jnp.float32),
+            pltpu.VMEM((2, high, LANES), jnp.float32),
+            pltpu.VMEM((2, 2, 2 * LANES, LANES), jnp.float32),
             pltpu.VMEM((chunk, LANES, LANES), jnp.float32),
             pltpu.VMEM((tall * deep, LANES), jnp.float32),
             pltpu.VMEM((high, LANES), jnp.float32),

time: 21.9 us -> 20.7 us (0.945)
  Pallas kernels: 21.7 us -> 20.5 us
    pallas_call x1, Pallas kernels: 20.5 us -> 19.3 us  [per_device(): pl.pallas_call(functools.partial(kernel, (rows, width, count, count_in, t...]
where the time goes in v2:
time: 20.7 us; the launch traced here: 20.5 us
  Pallas kernels  20.5 us (99%)
    pallas_call x1, Pallas kernels, per_device(): pl.pallas_call(functools.partial(kernel, (rows, width, count, count_in, t...  19.3 us
    pallas_call x1, Pallas kernels, per_device(): pl.pallas_call(functools.partial(spread, (rows, width)), out_shape=jax.Sh...  1.23 us

profile of v2, /device:TPU:5, one launch (start us, length us, event | category | flops | bytes accessed | tf_op | source)
XLA Modules:
  0.0 20.5 jit_solution(5164165481521612662)
XLA Ops:
  0.0 19.3 %shard_map.73.y_ref = f32[1024,128]{1,0:T(8,128)S(1)} custom-call(f32[16,128]{1,0:T(8,128)} %far_in.1, f32[16,128]{1,0:T(8,128)} %near_in.1, s32[16,128]{1,0:T(8,128)} %inline_in.1, s32[16,128]{1,0:T(8,128)} %time_in.1, s32[16]{0:T(128)} %low_in.1, s32[16]{0:T(128)} %high_in.1, s32[2]{0:T(128)} %strain_in.1), custom_call_target="tpu_custom_call" | custom-call | tf_op jit(solution)/shard_map/pallas_call | solution.py:488
  19.3 1.2 %shard_map.74 = f32[1024,128]{1,0:T(8,128)} custom-call(f32[1024,128]{1,0:T(8,128)S(1)} %shard_map.73.y_ref), custom_call_target="tpu_custom_call" | custom-call | tf_op jit(solution)/shard_map/pallas_call | solution.py:528

commit v3 on v2

--- a/solution.py
+++ b/solution.py
@@ -58,9 +58,11 @@
     far_ref,
     bound_ref,
     m_ref,
+    link_ref,
     packed_ref,
     loose_ref,
     enter_ref,
+    leave_ref,
     low_ref,
     high_ref,
     strain_ref,
@@ -309,10 +311,50 @@
             m_ref[t, c] = diff * diff + penalty
         return carry
 
+    def weight(kind, c, t):
+        return face_ref[c, pl.ds(kind * high + t, 1), :]
+
+    def update(t, here, before, across):
+        along = []
+        for c in range(chunk):
+            after = here[c + 1] if c < chunk - 1 else pltpu.roll(here[0], LANES - 1, 1)
+            along.append(weight(2, c, t) * (after - here[c]))
+        back = [pltpu.roll(along[-1], 1, 1)] + along[:-1]
+        for c in range(chunk):
+            m_ref[t, c] = (here[c] + (across[c] - before[c])) + (along[c] - back[c])
+
+    def link(t, here, ahead):
+        return [weight(1, c, t) * (ahead[c] - here[c]) for c in range(chunk)]
+
+    def row(t):
+        return [m_ref[t, c] for c in range(chunk)]
+
+    def relax(t, state):
+        here, before = state
+        ahead = row(t + 1)
+        across = link(t, here, ahead)
+        update(t, here, before, across)
+        return ahead, across
+
+    def sweep(start, stop, before=None):
+        here = row(start)
+        if before is None:
+            before = link(start - 1, row(start - 1), here)
+        return lax.fori_loop(start, stop, relax, (here, before), unroll=stop - start)
+
     for dj in (-1, 1):
         arrive(0, dj)
     prepare(0, (0,), [(REACH, REACH + rows - 1)])
     lax.fori_loop(REACH, REACH + rows, build, 0, unroll=4)
+
+    inner = min(2, (rows - 1) // 2)
+    for step in range(1, min(inner, ITERS) + 1):
+        start, stop = REACH + step, REACH + rows - step
+        first = link(start - 1, row(start - 1), row(start))
+        _, last_link = sweep(start, stop, first)
+        for c in range(chunk):
+            link_ref[0, step - 1, c] = first[c]
+            link_ref[1, step - 1, c] = last_link[c]
 
     for di, dj in OFFSETS:
         if di:
@@ -321,35 +363,40 @@
     lax.fori_loop(0, REACH, build, 0, unroll=5)
     lax.fori_loop(REACH + rows, tall, build, 0, unroll=5)
 
-    for step in range(1, ITERS + 1):
-        start, stop = step, tall - step
-
-        def relax(t, state):
-            here, before = state
-            along = []
-            for c in range(chunk):
-                after = here[c + 1] if c < chunk - 1 else pltpu.roll(here[0], LANES - 1, 1)
-                along.append(face_ref[c, pl.ds(2 * high + t, 1), :] * (after - here[c]))
-            back = [pltpu.roll(along[-1], 1, 1)] + along[:-1]
-            nexts, fluxes = [], []
-            for c in range(chunk):
-                ahead = m_ref[t + 1, c]
-                across = face_ref[c, pl.ds(high + t, 1), :] * (ahead - here[c])
-                m_ref[t, c] = (here[c] + (across - before[c])) + (along[c] - back[c])
-                nexts.append(ahead)
-                fluxes.append(across)
-            return nexts, fluxes
-
-        here = [m_ref[start, c] for c in range(chunk)]
-        before = [
-            face_ref[c, high + start - 1 : high + start, :] * (here[c] - m_ref[start - 1, c])
-            for c in range(chunk)
-        ]
-        lax.fori_loop(start, stop, relax, (here, before), unroll=stop - start)
-
+    for step in range(1, ITERS):
+        if step > inner:
+            sweep(step, tall - step)
+            continue
+        edge_row = REACH + step - 1
+        here, before = sweep(step, edge_row)
+        update(edge_row, here, before, [link_ref[0, step - 1, c] for c in range(chunk)])
+        first = [link_ref[1, step - 1, c] for c in range(chunk)]
+        sweep(REACH + rows - step, tall - step, first)
+
+    kept = range(REACH, REACH + rows)
+    back = {}
+    for t in kept:
+        along = weight(2, chunk - 1, t) * (
+            pltpu.roll(m_ref[t, 0], LANES - 1, 1) - m_ref[t, chunk - 1]
+        )
+        back[t] = (pltpu.roll(along, 1, 1), along)
     for c in range(chunk):
-        block = m_ref[REACH : REACH + rows, c].reshape(LANES, LANES)
-        packed_ref[c * LANES : (c + 1) * LANES, :] = jnp.transpose(block)
+        here = m_ref[REACH, c]
+        before = weight(1, c, REACH - 1) * (here - m_ref[REACH - 1, c])
+        fresh = []
+        for t in kept:
+            ahead = m_ref[t + 1, c]
+            across = weight(1, c, t) * (ahead - here)
+            if c < chunk - 1:
+                along = weight(2, c, t) * (m_ref[t, c + 1] - here)
+            else:
+                along = back[t][1]
+            fresh.append((here + (across - before)) + (along - back[t][0]))
+            back[t] = (along, back[t][1])
+            here, before = ahead, across
+        packed_ref[c * LANES : (c + 1) * LANES, :] = jnp.transpose(
+            jnp.concatenate(fresh, axis=0)
+        )
 
     def unpack(x):
         return [roll(x, -v) for v in range(GROUPS)]
@@ -376,9 +423,8 @@
 
         lax.fori_loop(REACH // chunk, (width + REACH - 1) // chunk + 1, loosen, 0)
 
-    last = width - 1
     state_copy = pltpu.make_async_remote_copy(
-        src_ref=y_ref.at[last * SUB : (last + 1) * SUB, :],
+        src_ref=leave_ref,
         dst_ref=enter_ref,
         send_sem=send_sem,
         recv_sem=recv_sem,
@@ -418,32 +464,44 @@
             x = s + REACH
             cost = unpack(packed_ref[pl.ds((x % chunk) * LANES + x // chunk, SUB, stride=PITCH), :])
             state = advance(state, cost, s // STRETCH)
-            if s < last:
-                for v in range(GROUPS):
-                    loose_ref[loose(s * GROUPS + v), :] = state[v]
-        y_ref[last * SUB : (last + 1) * SUB, :] = pack(state)
-
-    @pl.when(me > 0)
-    def _():
+            for v in range(GROUPS):
+                loose_ref[loose(s * GROUPS + v), :] = state[v]
+        leave_ref[...] = pack(state)
+
+    def follow(final):
         state_copy.wait_recv()
         state = unpack(enter_ref[...])
         for s in range(width):
-            cost = [loose_ref[loose((s + REACH) * GROUPS + v), :] for v in range(GROUPS)]
-            state = advance(state, cost, s // STRETCH)
-            y_ref[s * SUB : (s + 1) * SUB, :] = pack(state)
+            spots_s = [loose((s + REACH) * GROUPS + v) for v in range(GROUPS)]
+            state = advance(state, [loose_ref[spot, :] for spot in spots_s], s // STRETCH)
+            if final:
+                y_ref[s * SUB : (s + 1) * SUB, :] = pack(state)
+            else:
+                for v in range(GROUPS):
+                    loose_ref[loose(s * GROUPS + v), :] = state[v]
+        if not final:
+            leave_ref[...] = pack(state)
+
+    @pl.when((me > 0) & (me < count - 1))
+    def _():
+        follow(False)
+
+    @pl.when((me > 0) & (me == count - 1))
+    def _():
+        follow(True)
 
     @pl.when(me < count - 1)
     def _():
         state_copy.start()
 
-    @pl.when(me == 0)
+    @pl.when(me < count - 1)
     def _():
         def tighten(s, carry):
             x = [loose_ref[loose(s * GROUPS + v), :] for v in range(GROUPS)]
             y_ref[pl.ds(pl.multiple_of(s * SUB, SUB), SUB), :] = pack(x)
             return carry
 
-        lax.fori_loop(0, last, tighten, 0, unroll=4)
+        lax.fori_loop(0, width, tighten, 0, unroll=16)
 
     @pl.when(me < count - 1)
     def _():
@@ -457,20 +515,27 @@
                 copy.wait_send()
 
 
-def spread(dims, y_ref, out_ref, turned_ref):
+def spread(dims, y_ref, out_ref, ready_ref, sems):
     rows, width = dims
-    least = [None] * rows
+    blocks = [y_ref[pl.ds(g, width, stride=SUB), :] for g in range(SUB)]
+    low = jnp.transpose(functools.reduce(jnp.minimum, blocks))
+    least = [
+        jnp.min(low[r * SUB : (r + 1) * SUB], axis=0, keepdims=True) for r in range(rows)
+    ]
+    copies = []
     for g in range(SUB):
-        block = jnp.transpose(y_ref[pl.ds(g, width, stride=SUB), :])
-        turned_ref[g] = block
+        block = jnp.transpose(blocks[g])
         for r in range(rows):
-            tile = block[r * SUB : (r + 1) * SUB]
-            least[r] = tile if g == 0 else jnp.minimum(least[r], tile)
-    for r in range(rows):
-        low = jnp.min(least[r], axis=0, keepdims=True)
-        for g in range(SUB):
-            tile = turned_ref[g, r * SUB : (r + 1) * SUB, :] - low
-            out_ref[pl.ds(g * SUB * rows + r, SUB, stride=rows), :] = tile
+            ready_ref[pl.ds(g * SUB * rows + r, SUB, stride=rows), :] = (
+                block[r * SUB : (r + 1) * SUB] - least[r]
+            )
+        piece = pl.ds(g * SUB * rows, SUB * rows)
+        copies.append(
+            pltpu.make_async_copy(ready_ref.at[piece, :], out_ref.at[piece, :], sems.at[g])
+        )
+        copies[-1].start()
+    for copy in copies:
+        copy.wait()
 
 
 def per_device(near_trace, far_trace, inline_weight, time_weight, lag_low, lag_high, strain):
@@ -504,8 +569,10 @@
             pltpu.VMEM((tall * deep, LANES), jnp.float32),
             pltpu.VMEM((high, LANES), jnp.float32),
             pltpu.VMEM((tall, chunk, SUB, LANES), jnp.float32),
+            pltpu.VMEM((2, (rows - 1) // 2, chunk, SUB, LANES), jnp.float32),
             pltpu.VMEM((chunk * LANES, LANES), jnp.float32),
             pltpu.VMEM((chunk * PITCH * GROUPS * SUB, LANES), jnp.float32),
+            pltpu.VMEM((SUB, LANES), jnp.float32),
             pltpu.VMEM((SUB, LANES), jnp.float32),
             pltpu.SMEM(lag_low.shape, jnp.int32),
             pltpu.SMEM(lag_high.shape, jnp.int32),
@@ -529,8 +596,11 @@
         functools.partial(spread, (rows, width)),
         out_shape=jax.ShapeDtypeStruct((L * rows, width), jnp.float32),
         in_specs=[vmem],
-        out_specs=vmem,
-        scratch_shapes=[pltpu.VMEM((SUB, LANES, width), jnp.float32)],
+        out_specs=pl.BlockSpec(memory_space=pltpu.HBM),
+        scratch_shapes=[
+            pltpu.VMEM((L * rows, width), jnp.float32),
+            pltpu.SemaphoreType.DMA((SUB,)),
+        ],
         compiler_params=pltpu.CompilerParams(vmem_limit_bytes=24 << 20),
     )(packed)
     return out.reshape(L, rows, width)

time: 20.7 us -> 20 us (0.966)
  Pallas kernels: 20.5 us -> 19.8 us
    pallas_call x1, Pallas kernels: 19.3 us -> 18.8 us  [per_device(): pl.pallas_call(functools.partial(kernel, (rows, width, count, count_in, t...]
    pallas_call x1, Pallas kernels: 1.23 us -> 1.02 us  [per_device(): pl.pallas_call(functools.partial(spread, (rows, width)), out_shape=jax.Sh...]
where the time goes in v3:
time: 20 us; the launch traced here: 19.8 us
  Pallas kernels  19.8 us (99%)
    pallas_call x1, Pallas kernels, per_device(): pl.pallas_call(functools.partial(kernel, (rows, width, count, count_in, t...  18.8 us
    pallas_call x1, Pallas kernels, per_device(): pl.pallas_call(functools.partial(spread, (rows, width)), out_shape=jax.Sh...  1.02 us

profile of v3, /device:TPU:5, one launch (start us, length us, event | category | flops | bytes accessed | tf_op | source)
XLA Modules:
  0.0 19.8 jit_solution(5636331297732717673)
XLA Ops:
  0.0 18.8 %shard_map.73.y_ref = f32[1024,128]{1,0:T(8,128)S(1)} custom-call(f32[16,128]{1,0:T(8,128)} %far_in.1, f32[16,128]{1,0:T(8,128)} %near_in.1, s32[16,128]{1,0:T(8,128)} %inline_in.1, s32[16,128]{1,0:T(8,128)} %time_in.1, s32[16]{0:T(128)} %low_in.1, s32[16]{0:T(128)} %high_in.1, s32[2]{0:T(128)} %strain_in.1), custom_call_target="tpu_custom_call" | custom-call | tf_op jit(solution)/shard_map/pallas_call | solution.py:553
  18.8 1.0 %shard_map.74 = f32[1024,128]{1,0:T(8,128)} custom-call(f32[1024,128]{1,0:T(8,128)S(1)} %shard_map.73.y_ref), custom_call_target="tpu_custom_call" | custom-call | tf_op jit(solution)/shard_map/pallas_call | solution.py:595

commit v4 on v3

--- a/solution.py
+++ b/solution.py
@@ -225,34 +225,31 @@
     sizes = {-1: REACH, 0: rows, 1: REACH}
 
     def prepare(bank, parts, links):
-        gap = LANES // SHIFTS // SUB * SUB
-        far_at = dict(zip(parts, (0, -(-REACH // SUB) * SUB)))
-
         def place(ranges):
             spots, at = [], 0
             for start, stop in ranges:
-                at += (start - at) % SUB
                 spots.append((start, stop, at))
                 at += stop - start
-            assert at <= gap
-            return spots
-
-        cell_spots = place([(tops[di], tops[di] + sizes[di]) for di in parts])
-        link_spots = place(links)
-        for di, (_, _, at) in zip(parts, cell_spots):
-            top, size = tops[di], sizes[di]
+            return spots, at
+
+        cell_spots, unit = place([(tops[di], tops[di] + sizes[di]) for di in parts])
+        link_spots, used = place(links)
+        assert used <= unit and 6 * unit <= LANES
+        shifts = LANES // unit
+        for di, (top, stop, at) in zip(parts, cell_spots):
+            size = stop - top
             pair = windows(0, di)
-            for k in range(SHIFTS):
+            for k in range(shifts):
                 for tile, x in enumerate(ahead_by(*pair, k)):
-                    begin = k * gap + far_at[di]
+                    begin = k * unit + at
                     plain_ref[bank, 1, tile, begin : begin + size, :] = x
             for tile, x in enumerate(windows(1, di)):
                 plain_ref[bank, 0, tile, at : at + size, :] = x
             for tile, x in enumerate(windows(2, di)):
-                inline_ref[tile, top : top + size, :] = x
+                inline_ref[tile, top:stop, :] = x
             pair = windows(3, di)
             for tile, (x, y) in enumerate(zip(pair, ahead_by(*pair, 1))):
-                plain_ref[bank, 0, tile, 2 * gap + at : 2 * gap + at + size, :] = (
+                plain_ref[bank, 0, tile, 2 * unit + at : 2 * unit + at + size, :] = (
                     FACE_SCALE * jnp.minimum(x, y)
                 )
             if di:
@@ -262,10 +259,10 @@
                     x, y = marks[:, filled : filled + 1], marks[:, LANES - 1 : LANES]
                     low = x if low is None else jnp.maximum(low, x)
                     high_ = y if high_ is None else jnp.minimum(high_, y)
-                bound_ref[top : top + size, :] = jnp.where(line < LANES // 2, low, high_)
+                bound_ref[top:stop, :] = jnp.where(line < LANES // 2, low, high_)
         for start, stop, at in link_spots:
             for tile in range(2):
-                plain_ref[bank, 0, tile, gap + at : gap + at + stop - start, :] = (
+                plain_ref[bank, 0, tile, unit + at : unit + at + stop - start, :] = (
                     FACE_SCALE
                     * jnp.minimum(
                         inline_ref[tile, start:stop, :], inline_ref[tile, start + 1 : stop + 1, :]
@@ -276,27 +273,32 @@
                 field_ref[bank, kind, tile * LANES : (tile + 1) * LANES, :] = jnp.transpose(
                     plain_ref[bank, kind, tile]
                 )
-        for c in range(chunk):
-            piece = field_ref[bank, 0, pl.ds(c, PITCH, stride=chunk), :]
-            block = jnp.transpose(jnp.concatenate([piece] * GROUPS, axis=0))
-            for kind, spots in enumerate((cell_spots, link_spots, cell_spots)):
-                for start, stop, at in spots:
-                    face_ref[c, kind * high + start : kind * high + stop, :] = block[
-                        kind * gap + at : kind * gap + at + stop - start
-                    ]
-        for y in range(0, chunk + SUB - 1, SHIFTS):
+        for y in range(0, chunk + SUB - 1, shifts):
             pieces = [
                 field_ref[bank, 1, pl.ds(y + g * SUB, PITCH, stride=chunk), :]
                 for g in range(GROUPS)
             ]
             block = jnp.transpose(jnp.concatenate(pieces, axis=0))
-            for k in range(SHIFTS):
-                if y + k < deep:
-                    for di in parts:
-                        begin = k * gap + far_at[di]
-                        far_ref[pl.ds(tops[di] * deep + y + k, sizes[di], stride=deep), :] = (
-                            block[begin : begin + sizes[di]]
-                        )
+            for k in range(min(shifts, chunk + SUB - 1 - y)):
+                for start, stop, at in cell_spots:
+                    begin = k * unit + at
+                    far_ref[pl.ds(start * deep + y + k, stop - start, stride=deep), :] = block[
+                        begin : begin + stop - start
+                    ]
+        for c in range(0, chunk, 2):
+            pieces = [
+                field_ref[bank, 0, pl.ds(c + k, PITCH, stride=chunk), :]
+                for k in range(min(2, chunk - c))
+            ]
+            piece = jnp.where(line < 3 * unit, pieces[0], roll(pieces[-1], 3 * unit))
+            block = jnp.transpose(jnp.concatenate([piece] * GROUPS, axis=0))
+            for k in range(len(pieces)):
+                for kind, spots in enumerate((cell_spots, link_spots, cell_spots)):
+                    for start, stop, at in spots:
+                        begin = (3 * k + kind) * unit + at
+                        face_ref[c + k, kind * high + start : kind * high + stop, :] = block[
+                            begin : begin + stop - start
+                        ]
 
     sub = lax.broadcasted_iota(jnp.int32, (SUB, LANES), 0)
     lane = lax.broadcasted_iota(jnp.int32, (SUB, LANES), 1)
@@ -347,7 +349,7 @@
     prepare(0, (0,), [(REACH, REACH + rows - 1)])
     lax.fori_loop(REACH, REACH + rows, build, 0, unroll=4)
 
-    inner = min(2, (rows - 1) // 2)
+    inner = min(3, (rows - 1) // 2)
     for step in range(1, min(inner, ITERS) + 1):
         start, stop = REACH + step, REACH + rows - step
         first = link(start - 1, row(start - 1), row(start))
@@ -360,8 +362,8 @@
         if di:
             arrive(di, dj)
     prepare(1, (-1, 1), [(0, REACH), (REACH + rows - 1, tall - 1)])
-    lax.fori_loop(0, REACH, build, 0, unroll=5)
-    lax.fori_loop(REACH + rows, tall, build, 0, unroll=5)
+    lax.fori_loop(0, REACH, build, 0, unroll=REACH)
+    lax.fori_loop(REACH + rows, tall, build, 0, unroll=REACH)
 
     for step in range(1, ITERS):
         if step > inner:
@@ -473,13 +475,18 @@
         state = unpack(enter_ref[...])
         for s in range(width):
             spots_s = [loose((s + REACH) * GROUPS + v) for v in range(GROUPS)]
+            former = state
             state = advance(state, [loose_ref[spot, :] for spot in spots_s], s // STRETCH)
-            if final:
-                y_ref[s * SUB : (s + 1) * SUB, :] = pack(state)
+            if final and s:
+                y_ref[(s - 1) * SUB : s * SUB, :] = pack(former)
+            elif final:
+                continue
             else:
                 for v in range(GROUPS):
                     loose_ref[loose(s * GROUPS + v), :] = state[v]
-        if not final:
+        if final:
+            y_ref[(width - 1) * SUB : width * SUB, :] = pack(state)
+        else:
             leave_ref[...] = pack(state)
 
     @pl.when((me > 0) & (me < count - 1))

time: 20 us -> 20 us (level)
  no operation moved by 1% of the time
where the time goes in v4:
time: 20 us; the launch traced here: 19.8 us
  Pallas kernels  19.8 us (99%)
    pallas_call x1, Pallas kernels, per_device(): pl.pallas_call(functools.partial(kernel, (rows, width, count, count_in, t...  18.8 us
    pallas_call x1, Pallas kernels, per_device(): pl.pallas_call(functools.partial(spread, (rows, width)), out_shape=jax.Sh...  1.02 us

profile of v4, /device:TPU:5, one launch (start us, length us, event | category | flops | bytes accessed | tf_op | source)
XLA Modules:
  0.0 19.8 jit_solution(9284975380481056238)
XLA Ops:
  0.0 18.8 %shard_map.73.y_ref = f32[1024,128]{1,0:T(8,128)S(1)} custom-call(f32[16,128]{1,0:T(8,128)} %far_in.1, f32[16,128]{1,0:T(8,128)} %near_in.1, s32[16,128]{1,0:T(8,128)} %inline_in.1, s32[16,128]{1,0:T(8,128)} %time_in.1, s32[16]{0:T(128)} %low_in.1, s32[16]{0:T(128)} %high_in.1, s32[2]{0:T(128)} %strain_in.1), custom_call_target="tpu_custom_call" | custom-call | tf_op jit(solution)/shard_map/pallas_call | solution.py:560
  18.8 1.0 %shard_map.74 = f32[1024,128]{1,0:T(8,128)} custom-call(f32[1024,128]{1,0:T(8,128)S(1)} %shard_map.73.y_ref), custom_call_target="tpu_custom_call" | custom-call | tf_op jit(solution)/shard_map/pallas_call | solution.py:602
